TPU v7x, 256 devices: a whole 4x4x8 slice. The times are simulated.
256 devices in a mesh: ta: 4 (over x_lo, core), ha: 4 (over y), wa: 16 (over x_hi, z).
Axes of the slice: x: 4 (x_hi: 2, x_lo: 2; x = x_hi * 2 + x_lo), y: 4, z: 8, core: 2. Of those that a mesh axis runs over, the one named last changes fastest.
Arguments:
- queries: bfloat16 [8, 64, 128, 2048], P('ta', 'ha', 'wa'), may hold values from -16 to 16
- keyvals: bfloat16 [2, 8, 64, 128, 2048], P(None, 'ta', 'ha', 'wa'), may hold values from -6 to 6
- far_frames: int32 [8, 8, 16, 2], P('ta', 'ha', 'wa'), may hold values from 0 to 7, as said below
Outputs:
- attended: bfloat16 [8, 64, 128, 2048], P('ta', 'ha', 'wa')
Inputs may be any that keep to these rules, and one draw needn't show every extreme that they name: far_frames[t, a, b, :] are 2 different frames, each at a distance of 2 or more from t modulo 8.
All inputs are finite; a program needn't handle non-finite values.
Results may differ from a plain program's by a relative error of at most 0.0049.
Values may be sent and summed in bfloat16 or wider, within the bound.
A program may use at most 192 MiB of HBM per device.

v0:
```python
import jax
import jax.numpy as jnp
from jax import lax
from jax.sharding import PartitionSpec as P

TILE = 8
HEADS = 16
HD = 128
NFAR = 2


def extended_2(cells, sides, width, closed):
    for axis, dim in sides:
        count = lax.axis_size(axis)
        ends = count if closed else count - 1
        head = lax.slice_in_dim(cells, 0, width, axis=dim)
        tail = lax.slice_in_dim(cells, cells.shape[dim] - width, cells.shape[dim], axis=dim)
        cells = jnp.concatenate(
            [
                lax.ppermute(tail, axis, [(i, (i + 1) % count) for i in range(ends)]),
                cells,
                lax.ppermute(head, axis, [((i + 1) % count, i) for i in range(ends)]),
            ],
            axis=dim,
        )
    return cells


def start_at(*values):
    return tuple((jnp.asarray(value).astype(jnp.int32) for value in values))


def widen_space(timed):
    return extended_2(timed, (("ha", 2), ("wa", 3)), TILE, False)


def per_device(queries, keyvals, far_frames):
    frame_count, row_count, column_count, features = queries.shape
    tile_count = row_count // TILE
    scaling = HD ** (-0.5)
    wanted = far_frames[:, :, 0, :]
    shard_rows = lax.all_gather(keyvals, "ta", axis=1, tiled=True)
    piece_count = shard_rows.shape[1]
    frame_ids = jnp.arange(piece_count, dtype=jnp.int32)
    matches = (wanted[:, :, :, None] == frame_ids).astype(jnp.bfloat16)
    blocks = shard_rows.reshape(2, piece_count, tile_count, TILE, column_count, features)
    chosen = jnp.einsum("fanp,kpatwc->kfantwc", matches, blocks, preferred_element_type=jnp.float32)
    far_blocks = chosen.astype(jnp.bfloat16)
    timed = extended_2(keyvals, (("ta", 1),), 1, True)
    extended = widen_space(timed)
    row_base = lax.axis_index("ha") * tile_count
    row_limit = tile_count * lax.axis_size("ha")
    column_tile = lax.axis_index("wa")
    column_limit = lax.axis_size("wa")
    offsets = jnp.arange(3 * TILE, dtype=jnp.int32) // TILE - 1
    column_valid = (column_tile + offsets >= 0) & (column_tile + offsets < column_limit)

    def attend(tile_index):
        frame_at = tile_index // tile_count
        tile_at = tile_index % tile_count
        query_rows = lax.dynamic_slice(
            queries, start_at(frame_at, tile_at * TILE, 0, 0), (1, TILE, column_count, features)
        ).reshape(-1, HEADS, HD)
        window = lax.dynamic_slice(
            extended,
            start_at(0, frame_at, tile_at * TILE, 0, 0),
            (2, 3, 3 * TILE, column_count + 2 * TILE, features),
        )
        distant = lax.dynamic_slice(
            far_blocks,
            start_at(0, frame_at, tile_at, 0, 0, 0, 0),
            (2, 1, 1, NFAR, TILE, column_count, features),
        )
        near_keys = window[0].reshape(-1, HEADS, HD)
        near_values = window[1].reshape(-1, HEADS, HD)
        far_keys = distant[0].reshape(-1, HEADS, HD)
        far_values = distant[1].reshape(-1, HEADS, HD)
        row_valid = (row_base + tile_at + offsets >= 0) & (row_base + tile_at + offsets < row_limit)
        inside = jnp.broadcast_to(
            row_valid[None, :, None] & column_valid[None, None, :],
            (3, 3 * TILE, column_count + 2 * TILE),
        ).reshape(-1)
        near_scores = (
            jnp.einsum("qhd,khd->hqk", query_rows, near_keys, preferred_element_type=jnp.float32)
            * scaling
        )
        near_scores = jnp.where(inside[None, None, :], near_scores, jnp.float32(-1e30))
        far_scores = (
            jnp.einsum("qhd,khd->hqk", query_rows, far_keys, preferred_element_type=jnp.float32)
            * scaling
        )
        peak_score = jnp.maximum(
            jnp.max(near_scores, axis=-1, keepdims=True),
            jnp.max(far_scores, axis=-1, keepdims=True),
        )
        near_exp = jnp.exp(near_scores - peak_score)
        far_exp = jnp.exp(far_scores - peak_score)
        denominator = jnp.sum(near_exp, axis=-1, keepdims=True) + jnp.sum(
            far_exp, axis=-1, keepdims=True
        )
        near_normed = (near_exp / denominator).astype(jnp.bfloat16)
        far_normed = (far_exp / denominator).astype(jnp.bfloat16)
        blended = jnp.einsum(
            "hqk,khd->qhd", near_normed, near_values, preferred_element_type=jnp.float32
        )
        blended = blended + jnp.einsum(
            "hqk,khd->qhd", far_normed, far_values, preferred_element_type=jnp.float32
        )
        return blended.reshape(TILE, column_count, features).astype(jnp.bfloat16)

    tile_outputs = lax.map(attend, jnp.arange(frame_count * tile_count, dtype=jnp.int32))
    return tile_outputs.reshape(frame_count, row_count, column_count, features)


def solution(mesh):
    placed = (P("ta", "ha", "wa", None), P(None, "ta", "ha", "wa", None), P("ta", "ha", "wa", None))
    return jax.shard_map(
        per_device, mesh=mesh, in_specs=placed, out_specs=P("ta", "ha", "wa", None), check_vma=False
    )
```

profile of v0, /device:TPU:1, one launch (start us, length us, event | category | flops | bytes accessed | tf_op | source)
XLA Modules:
  0.0 539.9 jit_solution(11685587330300851445)
XLA Ops:
  6.5 1.8 fusion.41
  8.4 2.7 collective-permute-start
  11.0 0.7 collective-permute-start.1
  11.8 19.6 %collective-permute-done = bf16[2,1,16,8,2048]{4,3,2,1,0:T(8,128)(2,1)S(1)} collective-permute-done((bf16[2,1,16,8,2048]{4,3,2,1,0:T(8,128)(2,1)S(1)}, bf16[2,1,16,8,2048]{4,3,2,1,0:T(8,128)(2,1)S(1)}, u32[]{:S(2)}, u32[]{:S(2)}) %collective-permute-start) | collective-permute-done | bytes 1048608 | tf_op jit(solution)/shard_map/ppermute | solution.py:20
  31.6 5.1 collective-permute-done.1
  36.8 2.1 copy-done
  38.8 2.6 fusion.40
  41.4 1.3 collective-permute-start.3
  42.7 5.3 collective-permute-start.2
  48.1 42.1 %collective-permute-done.3 = bf16[2,4,8,8,2048]{4,3,2,1,0:T(8,128)(2,1)S(1)} collective-permute-done((bf16[2,4,8,8,2048]{4,3,2,1,0:T(8,128)(2,1)}, bf16[2,4,8,8,2048]{4,3,2,1,0:T(8,128)(2,1)S(1)}, u32[]{:S(2)}, u32[]{:S(2)}) %collective-permute-start.3) | collective-permute-done | bytes 2097184 | tf_op jit(solution)/shard_map/ppermute | solution.py:22
  90.2 0.9 collective-permute-done.2
  91.0 6.7 %pad_maximum_fusion.1 = bf16[2,4,32,8,2048]{4,3,2,1,0:T(8,128)(2,1)} fusion(bf16[2,4,8,8,2048]{4,3,2,1,0:T(8,128)(2,1)S(1)} %collective-permute-done.3, bf16[2,4,16,8,2048]{4,3,2,1,0:T(8,128)(2,1)} %copy-done, bf16[2,4,8,8,2048]{4,3,2,1,0:T(8,128)(2,1)} %collective-permute-done.2), kind=kLoop, calls=%fused_computation.46 | loop fusion | flops 8388608 | bytes 16777216 | tf_op jit(solution)/shard_map/concatenate | solution.py:18
  97.7 1.3 collective-permute-start.5
  99.0 7.2 %collective-permute-start.4 = (bf16[2,4,32,8,2048]{4,3,2,1,0:T(8,128)(2,1)}, bf16[2,4,32,8,2048]{4,3,2,1,0:T(8,128)(2,1)}, u32[]{:S(2)}, u32[]{:S(2)}) collective-permute-start(bf16[2,4,32,8,2048]{4,3,2,1,0:T(8,128)(2,1)} %pad_maximum_fusion.1), channel_id=1, source_target_pairs={{0,1},{1,2},{2,3},{3,4},{4,5},{5,6},{6,7},{7,8},{8,9},{9,10},{10,1... | collective-permute-start | bytes 25165832 | tf_op jit(solution)/shard_map/ppermute | solution.py:20
  106.2 173.8 %collective-permute-done.5 = bf16[2,4,32,8,2048]{4,3,2,1,0:T(8,128)(2,1)} collective-permute-done((bf16[2,4,32,8,2048]{4,3,2,1,0:T(8,128)(2,1)}, bf16[2,4,32,8,2048]{4,3,2,1,0:T(8,128)(2,1)}, u32[]{:S(2)}, u32[]{:S(2)}) %collective-permute-start.5) | collective-permute-done | bytes 8388640 | tf_op jit(solution)/shard_map/ppermute | solution.py:22
  280.0 0.9 collective-permute-done.4
  280.9 21.8 %pad_maximum_fusion = bf16[2,4,32,24,2048]{4,3,2,1,0:T(8,128)(2,1)} fusion(bf16[2,4,32,8,2048]{4,3,2,1,0:T(8,128)(2,1)} %collective-permute-done.5, bf16[2,4,8,8,2048]{4,3,2,1,0:T(8,128)(2,1)S(1)} %collective-permute-done.3, bf16[2,4,16,8,2048]{4,3,2,1,0:T(8,128)(2,1)} %copy-done, bf16[2,4,8,8,2048]{4,3,2,1,0:T(8,128)(2,1)} %collective-permute-done.2, ...), kind=kLoop, calls=%fused_computation.45 | loop fusion | flops 125829120 | bytes 50331648 | tf_op jit(solution)/shard_map/concatenate | solution.py:18
  302.8 8.9 %all-gather.2.cloned.1.call-done = bf16[2,8,16,8,2048]{4,3,2,1,0:T(8,128)(2,1)} async-done(((bf16[2,2,16,8,2048]{4,3,2,1,0:T(8,128)(2,1)}), bf16[2,8,16,8,2048]{4,3,2,1,0:T(8,128)(2,1)}) %all-gather.2.cloned.1.call-update) | async-done | bytes 8388624 | tf_op jit(solution)/shard_map/all_gather | solution.py:42
  311.6 12.4 %fusion.32 = bf16[2,2,2,2,8,8,2048]{6,3,5,4,0,1,2:T(2,128)(2,1)} fusion(bf16[2,8,2,8,8,2048,1]{5,4,3,2,1,0,6:T(8,128)(2,1)} %bitcast.72, s32[2,2,2]{2,0,1:T(2,128)S(1)} %copy.13), kind=kOutput, calls=%fused_computation.50 | convolution fusion | flops 35651648 | bytes 12582944 | tf_op jit(solution)/shard_map/fanp,kpatwc->kfantwc/dot_general | solution.py:47
  324.0 209.1 %while.13 = (s32[]{:T(128)}, bf16[4,8,8,2048]{3,2,1,0:T(8,128)(2,1)}, s32[4]{0:T(128)S(1)}, bf16[2,4,32,24,2048]{4,3,2,1,0:T(8,128)(2,1)}, s32[]{:T(128)}, /*ind...) while((s32[]{:T(128)}, ...), condition=%wide.region_5.6_spmd.clone, body=%wide.region_0.5_spmd.clone.sunk | while | flops 995490816 | bytes 127479776 | solution.py:111
  324.0 0.6 dynamic_slice.33
  326.9 8.4 %constant_dynamic-slice_fusion.6 = (bf16[1,3,24,24,2048]{4,3,2,1,0:T(8,128)(2,1)}, bf16[1,3,24,24,2048]{4,3,2,1,0:T(8,128)(2,1)S(1)}) fusion(bf16[2,4,32,24,2048]{4,3,2,1,0:T(8,128)(2,1)} %get-tuple-element.294, s32[]{:T(128)S(6)} %select_n.118, s32[]{:T(128)S(6)} %select_n.120, s32[]{:T(128)S(6)} %add.155), kind=kLoop, calls=%fused_computation.35.clone.1 | loop fusion | bytes 28311564 | tf_op jit(solution)/shard_map/while/body/eval_jaxpr/slice | solution.py:74
  335.3 5.5 %copy.74 = bf16[216,8,16,128]{3,2,1,0:T(8,128)(2,1)} copy(bf16[216,8,16,128]{3,1,2,0:T(8,128)(2,1)S(1)} %bitcast.64) | data formatting | bytes 14155776 | tf_op jit(solution)/shard_map/while
  341.0 8.5 %copy.75 = bf16[216,8,16,128]{3,2,1,0:T(8,128)(2,1)} copy(bf16[216,8,16,128]{3,1,2,0:T(8,128)(2,1)} %bitcast.62) | data formatting | bytes 14155776 | tf_op jit(solution)/shard_map/while
  349.5 1.0 dynamic-slice_bitcast_fusion.2
  350.5 10.4 %fusion.52 = (f32[16,64]{1,0:T(8,128)S(1)}, f32[16,64,1728]{2,1,0:T(8,128)}) fusion(pred[1728]{0:T(1024)(128)(4,1)S(1)} %broadcast_in_dim.76, bf16[1728,16,128]{2,1,0:T(8,128)(2,1)} %bitcast.63, bf16[64,16,128]{2,1,0:T(8,128)(2,1)S(1)} %bitcast.66), kind=kOutput, calls=%fused_computation.9.clone.1 | convolution fusion | flops 458292224 | bytes 14423744 | tf_op jit(solution)/shard_map/while/body/eval_jaxpr/qhd,khd->hqk/dot_general | solution.py:84
  361.0 2.1 constant_dynamic-slice_fusion.7
  363.4 0.6 fusion.53
  363.9 4.4 fusion.54
  368.8 5.6 %fusion.56 = f32[16,128,64]{1,2,0:T(8,128)S(1)} fusion(bf16[1728,16,128]{2,1,0:T(8,128)(2,1)} %bitcast.65, f32[16,64,1728]{2,1,0:T(8,128)S(1)} %bitcast.61, f32[16,64]{1,0:T(8,128)S(1)} %add.160, f32[16,64]{1,0:T(8,128)S(1)} %max.13, pred[1728]{0:T(1024)(128)(4,1)S(1)} %broadcast_in_dim.76), kind=kOutput, calls=%fused_computation.5.clone.1 | convolution fusion | flops 461832192 | bytes 14689984 | tf_op jit(solution)/shard_map/while/body/eval_jaxpr/hqk,khd->qhd/dot_general | solution.py:103
  375.6 0.7 constant_dynamic-update-slice_fusion.5
  376.3 0.6 dynamic_slice.33
  379.2 8.4 %constant_dynamic-slice_fusion.6 = (bf16[1,3,24,24,2048]{4,3,2,1,0:T(8,128)(2,1)}, bf16[1,3,24,24,2048]{4,3,2,1,0:T(8,128)(2,1)S(1)}) fusion(bf16[2,4,32,24,2048]{4,3,2,1,0:T(8,128)(2,1)} %get-tuple-element.294, s32[]{:T(128)S(6)} %select_n.118, s32[]{:T(128)S(6)} %select_n.120, s32[]{:T(128)S(6)} %add.155), kind=kLoop, calls=%fused_computation.35.clone.1 | loop fusion | bytes 28311564 | tf_op jit(solution)/shard_map/while/body/eval_jaxpr/slice | solution.py:74
  387.6 5.5 %copy.74 = bf16[216,8,16,128]{3,2,1,0:T(8,128)(2,1)} copy(bf16[216,8,16,128]{3,1,2,0:T(8,128)(2,1)S(1)} %bitcast.64) | data formatting | bytes 14155776 | tf_op jit(solution)/shard_map/while
  393.3 8.5 %copy.75 = bf16[216,8,16,128]{3,2,1,0:T(8,128)(2,1)} copy(bf16[216,8,16,128]{3,1,2,0:T(8,128)(2,1)} %bitcast.62) | data formatting | bytes 14155776 | tf_op jit(solution)/shard_map/while
  401.8 1.0 dynamic-slice_bitcast_fusion.2
  402.8 10.4 %fusion.52 = (f32[16,64]{1,0:T(8,128)S(1)}, f32[16,64,1728]{2,1,0:T(8,128)}) fusion(pred[1728]{0:T(1024)(128)(4,1)S(1)} %broadcast_in_dim.76, bf16[1728,16,128]{2,1,0:T(8,128)(2,1)} %bitcast.63, bf16[64,16,128]{2,1,0:T(8,128)(2,1)S(1)} %bitcast.66), kind=kOutput, calls=%fused_computation.9.clone.1 | convolution fusion | flops 458292224 | bytes 14423744 | tf_op jit(solution)/shard_map/while/body/eval_jaxpr/qhd,khd->hqk/dot_general | solution.py:84
  413.2 2.1 constant_dynamic-slice_fusion.7
  415.6 0.6 fusion.53
  416.2 4.4 fusion.54
  421.1 5.6 %fusion.56 = f32[16,128,64]{1,2,0:T(8,128)S(1)} fusion(bf16[1728,16,128]{2,1,0:T(8,128)(2,1)} %bitcast.65, f32[16,64,1728]{2,1,0:T(8,128)S(1)} %bitcast.61, f32[16,64]{1,0:T(8,128)S(1)} %add.160, f32[16,64]{1,0:T(8,128)S(1)} %max.13, pred[1728]{0:T(1024)(128)(4,1)S(1)} %broadcast_in_dim.76), kind=kOutput, calls=%fused_computation.5.clone.1 | convolution fusion | flops 461832192 | bytes 14689984 | tf_op jit(solution)/shard_map/while/body/eval_jaxpr/hqk,khd->qhd/dot_general | solution.py:103
  427.8 0.7 constant_dynamic-update-slice_fusion.5
  428.6 0.6 dynamic_slice.33
  431.5 8.4 %constant_dynamic-slice_fusion.6 = (bf16[1,3,24,24,2048]{4,3,2,1,0:T(8,128)(2,1)}, bf16[1,3,24,24,2048]{4,3,2,1,0:T(8,128)(2,1)S(1)}) fusion(bf16[2,4,32,24,2048]{4,3,2,1,0:T(8,128)(2,1)} %get-tuple-element.294, s32[]{:T(128)S(6)} %select_n.118, s32[]{:T(128)S(6)} %select_n.120, s32[]{:T(128)S(6)} %add.155), kind=kLoop, calls=%fused_computation.35.clone.1 | loop fusion | bytes 28311564 | tf_op jit(solution)/shard_map/while/body/eval_jaxpr/slice | solution.py:74
  439.8 5.5 %copy.74 = bf16[216,8,16,128]{3,2,1,0:T(8,128)(2,1)} copy(bf16[216,8,16,128]{3,1,2,0:T(8,128)(2,1)S(1)} %bitcast.64) | data formatting | bytes 14155776 | tf_op jit(solution)/shard_map/while
  445.5 8.5 %copy.75 = bf16[216,8,16,128]{3,2,1,0:T(8,128)(2,1)} copy(bf16[216,8,16,128]{3,1,2,0:T(8,128)(2,1)} %bitcast.62) | data formatting | bytes 14155776 | tf_op jit(solution)/shard_map/while
  454.0 1.0 dynamic-slice_bitcast_fusion.2
  455.1 10.4 %fusion.52 = (f32[16,64]{1,0:T(8,128)S(1)}, f32[16,64,1728]{2,1,0:T(8,128)}) fusion(pred[1728]{0:T(1024)(128)(4,1)S(1)} %broadcast_in_dim.76, bf16[1728,16,128]{2,1,0:T(8,128)(2,1)} %bitcast.63, bf16[64,16,128]{2,1,0:T(8,128)(2,1)S(1)} %bitcast.66), kind=kOutput, calls=%fused_computation.9.clone.1 | convolution fusion | flops 458292224 | bytes 14423744 | tf_op jit(solution)/shard_map/while/body/eval_jaxpr/qhd,khd->hqk/dot_general | solution.py:84
  465.5 2.1 constant_dynamic-slice_fusion.7
  467.9 0.6 fusion.53
  468.5 4.4 fusion.54
  473.4 5.6 %fusion.56 = f32[16,128,64]{1,2,0:T(8,128)S(1)} fusion(bf16[1728,16,128]{2,1,0:T(8,128)(2,1)} %bitcast.65, f32[16,64,1728]{2,1,0:T(8,128)S(1)} %bitcast.61, f32[16,64]{1,0:T(8,128)S(1)} %add.160, f32[16,64]{1,0:T(8,128)S(1)} %max.13, pred[1728]{0:T(1024)(128)(4,1)S(1)} %broadcast_in_dim.76), kind=kOutput, calls=%fused_computation.5.clone.1 | convolution fusion | flops 461832192 | bytes 14689984 | tf_op jit(solution)/shard_map/while/body/eval_jaxpr/hqk,khd->qhd/dot_general | solution.py:103
  480.1 0.7 constant_dynamic-update-slice_fusion.5
  480.8 0.6 dynamic_slice.33
  483.7 8.4 %constant_dynamic-slice_fusion.6 = (bf16[1,3,24,24,2048]{4,3,2,1,0:T(8,128)(2,1)}, bf16[1,3,24,24,2048]{4,3,2,1,0:T(8,128)(2,1)S(1)}) fusion(bf16[2,4,32,24,2048]{4,3,2,1,0:T(8,128)(2,1)} %get-tuple-element.294, s32[]{:T(128)S(6)} %select_n.118, s32[]{:T(128)S(6)} %select_n.120, s32[]{:T(128)S(6)} %add.155), kind=kLoop, calls=%fused_computation.35.clone.1 | loop fusion | bytes 28311564 | tf_op jit(solution)/shard_map/while/body/eval_jaxpr/slice | solution.py:74
  492.1 5.5 %copy.74 = bf16[216,8,16,128]{3,2,1,0:T(8,128)(2,1)} copy(bf16[216,8,16,128]{3,1,2,0:T(8,128)(2,1)S(1)} %bitcast.64) | data formatting | bytes 14155776 | tf_op jit(solution)/shard_map/while
  497.8 8.5 %copy.75 = bf16[216,8,16,128]{3,2,1,0:T(8,128)(2,1)} copy(bf16[216,8,16,128]{3,1,2,0:T(8,128)(2,1)} %bitcast.62) | data formatting | bytes 14155776 | tf_op jit(solution)/shard_map/while
  506.3 1.0 dynamic-slice_bitcast_fusion.2
  507.3 10.4 %fusion.52 = (f32[16,64]{1,0:T(8,128)S(1)}, f32[16,64,1728]{2,1,0:T(8,128)}) fusion(pred[1728]{0:T(1024)(128)(4,1)S(1)} %broadcast_in_dim.76, bf16[1728,16,128]{2,1,0:T(8,128)(2,1)} %bitcast.63, bf16[64,16,128]{2,1,0:T(8,128)(2,1)S(1)} %bitcast.66), kind=kOutput, calls=%fused_computation.9.clone.1 | convolution fusion | flops 458292224 | bytes 14423744 | tf_op jit(solution)/shard_map/while/body/eval_jaxpr/qhd,khd->hqk/dot_general | solution.py:84
  517.8 2.1 constant_dynamic-slice_fusion.7
  520.2 0.6 fusion.53
  520.8 4.4 fusion.54
  525.7 5.6 %fusion.56 = f32[16,128,64]{1,2,0:T(8,128)S(1)} fusion(bf16[1728,16,128]{2,1,0:T(8,128)(2,1)} %bitcast.65, f32[16,64,1728]{2,1,0:T(8,128)S(1)} %bitcast.61, f32[16,64]{1,0:T(8,128)S(1)} %add.160, f32[16,64]{1,0:T(8,128)S(1)} %max.13, pred[1728]{0:T(1024)(128)(4,1)S(1)} %broadcast_in_dim.76), kind=kOutput, calls=%fused_computation.5.clone.1 | convolution fusion | flops 461832192 | bytes 14689984 | tf_op jit(solution)/shard_map/while/body/eval_jaxpr/hqk,khd->qhd/dot_general | solution.py:103
  532.4 0.7 constant_dynamic-update-slice_fusion.5
  (93 shorter events, 8.1 us)
Async XLA Ops:
  6.5 24.9 %copy-start.1 = (bf16[2,2,16,8,2048]{4,3,2,1,0:T(8,128)(2,1)S(1)}, bf16[2,2,16,8,2048]{4,3,2,1,0:T(8,128)(2,1)}, u32[]{:S(2)}) copy-start(bf16[2,2,16,8,2048]{4,3,2,1,0:T(8,128)(2,1)} %param.6) | copy-start | bytes 6291460
  6.5 305.1 %all-gather.2.cloned.1.call-start = ((), (), s32[]{:S(2)}) async-start(), calls=%async_computation | async-start | bytes 10485760 | tf_op jit(solution)/shard_map/all_gather | solution.py:42
  8.4 23.0 %collective-permute-start = (bf16[2,1,16,8,2048]{4,3,2,1,0:T(8,128)(2,1)S(1)}, bf16[2,1,16,8,2048]{4,3,2,1,0:T(8,128)(2,1)S(1)}, u32[]{:S(2)}, u32[]{:S(2)}) collective-permute-start(bf16[2,1,16,8,2048]{4,3,2,1,0:T(8,128)(2,1)S(1)} %get-tuple-element.187), channel_id=1, source_target_pairs={{0,64},{64,128},{128,192},{192,0},{1,65},{65,129},{129,193},{193,1... | collective-permute-start | bytes 3145736 | tf_op jit(solution)/shard_map/ppermute | solution.py:20
  11.0 25.6 %collective-permute-start.1 = (bf16[2,1,16,8,2048]{4,3,2,1,0:T(8,128)(2,1)S(1)}, bf16[2,1,16,8,2048]{4,3,2,1,0:T(8,128)(2,1)S(1)}, u32[]{:S(2)}, u32[]{:S(2)}) collective-permute-start(bf16[2,1,16,8,2048]{4,3,2,1,0:T(8,128)(2,1)S(1)} %get-tuple-element.186), channel_id=1, source_target_pairs={{64,0},{128,64},{192,128},{0,192},{65,1},{129,65},{193,129},{1,193... | collective-permute-start | bytes 3145736 | tf_op jit(solution)/shard_map/ppermute | solution.py:22
  36.8 2.1 copy-start
  41.4 48.7 %collective-permute-start.3 = (bf16[2,4,8,8,2048]{4,3,2,1,0:T(8,128)(2,1)}, bf16[2,4,8,8,2048]{4,3,2,1,0:T(8,128)(2,1)S(1)}, u32[]{:S(2)}, u32[]{:S(2)}) collective-permute-start(bf16[2,4,8,8,2048]{4,3,2,1,0:T(8,128)(2,1)} %get-tuple-element.185), channel_id=1, source_target_pairs={{16,0},{32,16},{48,32},{17,1},{33,17},{49,33},{18,2},{34,18},{50,3... | collective-permute-start | bytes 6291464 | tf_op jit(solution)/shard_map/ppermute | solution.py:22
  42.7 48.3 %collective-permute-start.2 = (bf16[2,4,8,8,2048]{4,3,2,1,0:T(8,128)(2,1)}, bf16[2,4,8,8,2048]{4,3,2,1,0:T(8,128)(2,1)}, u32[]{:S(2)}, u32[]{:S(2)}) collective-permute-start(bf16[2,4,8,8,2048]{4,3,2,1,0:T(8,128)(2,1)} %get-tuple-element.184), channel_id=1, source_target_pairs={{0,16},{16,32},{32,48},{1,17},{17,33},{33,49},{2,18},{18,34},{34,5... | collective-permute-start | bytes 6291464 | tf_op jit(solution)/shard_map/ppermute | solution.py:20
  48.0 58.2 %copy-start.2 = (s32[2,2,1,2]{3,2,1,0:T(1,128)S(1)}, s32[2,2,1,2]{3,2,1,0:T(1,128)}, u32[]{:S(2)}) copy-start(s32[2,2,1,2]{3,2,1,0:T(1,128)} %param.7) | copy-start | bytes 100
  97.7 182.4 %collective-permute-start.5 = (bf16[2,4,32,8,2048]{4,3,2,1,0:T(8,128)(2,1)}, bf16[2,4,32,8,2048]{4,3,2,1,0:T(8,128)(2,1)}, u32[]{:S(2)}, u32[]{:S(2)}) collective-permute-start(bf16[2,4,32,8,2048]{4,3,2,1,0:T(8,128)(2,1)} %pad_maximum_fusion.1), channel_id=1, source_target_pairs={{1,0},{2,1},{3,2},{4,3},{5,4},{6,5},{7,6},{8,7},{9,8},{10,9},{11,1... | collective-permute-start | bytes 25165832 | tf_op jit(solution)/shard_map/ppermute | solution.py:22
  99.0 182.0 %collective-permute-start.4 = (bf16[2,4,32,8,2048]{4,3,2,1,0:T(8,128)(2,1)}, bf16[2,4,32,8,2048]{4,3,2,1,0:T(8,128)(2,1)}, u32[]{:S(2)}, u32[]{:S(2)}) collective-permute-start(bf16[2,4,32,8,2048]{4,3,2,1,0:T(8,128)(2,1)} %pad_maximum_fusion.1), channel_id=1, source_target_pairs={{0,1},{1,2},{2,3},{3,4},{4,5},{5,6},{6,7},{7,8},{8,9},{9,10},{10,1... | collective-permute-start | bytes 25165832 | tf_op jit(solution)/shard_map/ppermute | solution.py:20
  361.0 7.9 %slice-start = ((s8[7340032]{0:T(1024)(128)(4,1)}), s8[3145728]{0:T(1024)(128)(4,1)S(1)}, s32[]{:S(2)}) async-start(s8[7340032]{0:T(1024)(128)(4,1)} %bitcast.60), calls=%async_computation.1 | async-start | bytes 6291456 | tf_op jit(solution)/shard_map/while
  363.9 4.9 slice-start.1
  413.2 7.9 %slice-start = ((s8[7340032]{0:T(1024)(128)(4,1)}), s8[3145728]{0:T(1024)(128)(4,1)S(1)}, s32[]{:S(2)}) async-start(s8[7340032]{0:T(1024)(128)(4,1)} %bitcast.60), calls=%async_computation.1 | async-start | bytes 6291456 | tf_op jit(solution)/shard_map/while
  416.2 4.9 slice-start.1
  465.5 7.9 %slice-start = ((s8[7340032]{0:T(1024)(128)(4,1)}), s8[3145728]{0:T(1024)(128)(4,1)S(1)}, s32[]{:S(2)}) async-start(s8[7340032]{0:T(1024)(128)(4,1)} %bitcast.60), calls=%async_computation.1 | async-start | bytes 6291456 | tf_op jit(solution)/shard_map/while
  468.5 4.9 slice-start.1
  517.8 7.9 %slice-start = ((s8[7340032]{0:T(1024)(128)(4,1)}), s8[3145728]{0:T(1024)(128)(4,1)S(1)}, s32[]{:S(2)}) async-start(s8[7340032]{0:T(1024)(128)(4,1)} %bitcast.60), calls=%async_computation.1 | async-start | bytes 6291456 | tf_op jit(solution)/shard_map/while
  520.8 4.9 slice-start.1
Sparse Core Ops, SparseCore 0:
  48.2 263.4 all-gather.1
where the time goes:
time: 545 us; the launch traced here: 540 us
  waiting for transfers between devices  251 us (46%)
  local copies, waits for them, and re-layouts  118 us (22%)
  matrix products  80.8 us (15%)
  other arithmetic  48.3 us (9%)
  starting transfers between devices  18.5 us (3%)
  between operations  13.5 us (2%)
  loops' own time  9.89 us (2%)
    ppermute x3, waiting for transfers between devices, extended_2(): lax.ppermute(head, axis, [((i + 1) % count, i) for i in range(ends)])  221 us
    while x48, local copies, waits for them, and re-layouts  62.2 us
    dot_general x4, matrix products, attend(): jnp.einsum('qhd,khd->hqk', query_rows, near_keys, preferred_element_type=...  41.8 us
    slice x4, local copies, waits for them, and re-layouts, attend(): near_keys = window[0].reshape(-1, HEADS, HD)  33.5 us
    concatenate x2, other arithmetic, extended_2(): jnp.concatenate([lax.ppermute(tail, axis, [(i, (i + 1) % count) for i in...  28.5 us
    dot_general x4, matrix products, attend(): jnp.einsum('hqk,khd->qhd', near_normed, near_values, preferred_element_ty...  22.6 us
    ppermute x3, waiting for transfers between devices, extended_2(): lax.ppermute(tail, axis, [(i, (i + 1) % count) for i in range(ends)])  21.4 us
    reduce_sum x4, other arithmetic, attend(): jnp.sum(near_exp, axis=-1, keepdims=True)  17.8 us
  transfers between devices with their start and end apart: 7, of which 7 were waited for; matrix products, arithmetic and copies ran while one was open for 5% of the time, Pallas kernels for 0%

commit v1 on v0

v1 whole, which is shorter than its diff:
```python
import functools

import jax
import jax.numpy as jnp
from jax import lax
from jax.experimental import pallas as pl
from jax.experimental.pallas import tpu as pltpu
from jax.sharding import PartitionSpec as P

MESH = pl.DeviceIdType.MESH
HD = 128
NF = 8
ROWS = 128
EXP2_SCALE = HD**-0.5 * 1.4426950408889634
NEG = -1e30
NT = (((1,), (1,)), ((), ()))


def kernel(q, kv, far, out, *scratch):
    qs, own, left, right = (scratch[4 * i : 4 * i + 4] for i in range(4))
    (fars, bias, scores, probs, result, kv_send, kv_recv, q_send, q_recv, f_send, f_recv, z_send, z_recv, o_send, o_recv) = scratch[16:]
    ta, y, wa = lax.axis_index("ta"), lax.axis_index("ha"), lax.axis_index("wa")
    x_lo, core, x_hi, z = ta // 2, ta % 2, wa // 8, wa % 8
    x = x_hi * 2 + x_lo
    column = core * 8 + z
    has_left, has_right = column > 0, column < 15

    def place(px, pcore, py):
        return {"ta": (px % 2) * 2 + pcore, "ha": py, "wa": (px // 2) * 8 + z}

    def source(pta, py):
        return {"ta": pta, "ha": py, "wa": core * 8 + z}

    def beside(side):
        c = column + side
        return {"ta": x_lo * 2 + c // 8, "ha": y, "wa": x_hi * 8 + c % 8}

    def lanes(head):
        return pl.ds(pl.multiple_of(head * HD, HD), HD)

    barrier = pltpu.get_barrier_semaphore()

    @pl.loop(0, 16)
    def _(i):
        for device in (place(i // 4, x_hi, i % 4), source(i // 4, i % 4)):
            pl.semaphore_signal(barrier, inc=1, device_id=device, device_id_type=MESH)

    for side, there in ((-1, has_left), (1, has_right)):

        @pl.when(there)
        def _(side=side):
            pl.semaphore_signal(barrier, inc=1, device_id=beside(side), device_id_type=MESH)

    pl.semaphore_wait(barrier, 32 + has_left.astype(jnp.int32) + has_right.astype(jnp.int32))

    def kv_copy(k, dx):
        px, py = (x + dx) % 4, (y + k) % 4
        return (kv.at[:, :, :, lanes(px * 4 + py)], own[k].at[:, pl.ds(2 * ta, 2)], kv_send.at[4 * k + dx], kv_recv.at[4 * k + ta], px, py)

    def q_copy(k, dx):
        px, py = (x + dx) % 4, (y + k) % 4
        return (q.at[:, :, lanes(px * 4 + py)], qs[k].at[pl.ds(2 * ta, 2)], q_send.at[4 * k + dx], q_recv.at[4 * k + ta], px, py)

    def far_copy(k, dx):
        px, py = (x + dx) % 4, (y + k) % 4
        return (far, fars.at[4 * k + ta], f_send.at[4 * k + dx], f_recv.at[4 * k + ta], px, py)

    def remote(copy):
        src, dst, ss, rs, px, py = copy
        return pltpu.make_async_remote_copy(src, dst, ss, rs, device_id=place(px, x_hi, py), device_id_type=MESH)

    def exchange(make, k):
        src, dst, _, rs, _, _ = make(k, 0)
        if k == 0:

            @pl.when(core == x_hi)
            def _():
                pltpu.make_async_copy(src, dst, rs).start()

            @pl.when(core != x_hi)
            def _():
                remote(make(k, 0)).start()
        else:
            remote(make(k, 0)).start()

        @pl.loop(1, 4)
        def _(dx):
            remote(make(k, dx)).start()

    def exchanged(make, k):
        if k == 0:

            @pl.when(core != x_hi)
            def _():
                remote(make(k, 0)).wait_send()
        else:
            remote(make(k, 0)).wait_send()

        @pl.loop(1, 4)
        def _(dx):
            remote(make(k, dx)).wait_send()

    for k in range(4):
        exchange(far_copy, k)
    exchange(kv_copy, 0)
    exchange(kv_copy, 1)
    exchange(q_copy, 0)
    exchange(q_copy, 1)
    for k in (2, 3):
        exchange(kv_copy, k)
        exchange(q_copy, k)

    @pl.when(column == 0)
    def _():
        for ref in left:
            ref[...] = jnp.zeros_like(ref)

    @pl.when(column == 15)
    def _():
        for ref in right:
            ref[...] = jnp.zeros_like(ref)

    nearer = (((x - 2 * core + 3) % 4) < ((x - 2 * core + 4) % 4)).astype(jnp.int32)

    def piece(j):
        return ((nearer + j // 2) % 2) * 2 + j % 2

    def halo_copy(k, t, side):
        part = (slice(None), pl.ds(2 * t, 2))
        s = 0 if side < 0 else 1
        return pltpu.make_async_remote_copy(
            own[k].at[part],
            (right if side < 0 else left)[k].at[part],
            z_send.at[s, 4 * k + t],
            z_recv.at[s, 4 * k + t],
            device_id=beside(side),
            device_id_type=MESH,
        )

    def forward(k):
        @pl.loop(0, 4)
        def _(j):
            t = piece(j)
            pltpu.make_async_copy(own[k].at[:, pl.ds(2 * t, 2)], own[k].at[:, pl.ds(2 * t, 2)], kv_recv.at[4 * k + t]).wait()
            for side, there in ((1, has_right), (-1, has_left)):

                @pl.when(there)
                def _(side=side):
                    halo_copy(k, t, side).start()

    def arrived(k):
        @pl.loop(0, 4)
        def _(t):
            @pl.when(has_left)
            def _():
                halo_copy(k, t, 1).wait_recv()

            @pl.when(has_right)
            def _():
                halo_copy(k, t, -1).wait_recv()

            pltpu.make_async_copy(qs[k].at[pl.ds(2 * t, 2)], qs[k].at[pl.ds(2 * t, 2)], q_recv.at[4 * k + t]).wait()
            pltpu.make_async_copy(far, fars.at[4 * k + t], f_recv.at[4 * k + t]).wait()

    def set_bias(k):
        wraps = (y == k).astype(jnp.int32)
        row = lax.broadcasted_iota(jnp.int32, (ROWS, 2 * ROWS), 0)
        key = lax.broadcasted_iota(jnp.int32, (ROWS, 2 * ROWS), 1)
        half = row // 64
        base = jnp.where((key >= half * (64 + 64 * wraps)) & (key < 192 - 64 * wraps + half * 256), 0.0, NEG).astype(jnp.float32)
        bias[1] = base
        bias[0] = jnp.where(has_left, base, NEG)
        bias[2] = jnp.where(has_right, base, NEG)
        bias[3] = jnp.where(half == key // 128, 0.0, NEG).astype(jnp.float32)

    def unit(k, t):
        low = (k + 1) % 4
        query = jnp.concatenate([qs[low][t, 64:, :], qs[k][t, :64, :]], axis=0)
        around = [(t + 7) % NF, t, (t + 1) % NF]
        f_low, f_here = 4 * low + t // 2, 4 * k + t // 2
        f_at = (t % 2) * 4
        distant = [fars[f_low, f_at + 2], fars[f_low, f_at + 3], fars[f_here, f_at], fars[f_here, f_at + 1]]

        def rows(kind):
            chunks = []
            for side, cells in enumerate((left, own, right)):
                for f in around:
                    chunks.append((side, lambda cells=cells, f=f: jnp.concatenate([cells[low][kind, f], cells[k][kind, f]], axis=0)))
            chunks.append(
                (
                    3,
                    lambda: jnp.concatenate(
                        [
                            own[low][kind, distant[0], 64:, :],
                            own[low][kind, distant[1], 64:, :],
                            own[k][kind, distant[2], :64, :],
                            own[k][kind, distant[3], :64, :],
                        ],
                        axis=0,
                    ),
                )
            )
            return chunks

        peak = None
        for i, (side, load) in enumerate(rows(0)):
            s = lax.dot_general(query, load(), NT, preferred_element_type=jnp.float32) * EXP2_SCALE + bias[side]
            scores[:, 256 * i : 256 * i + 256] = s
            top = jnp.maximum(s[:, :128], s[:, 128:])
            peak = top if peak is None else jnp.maximum(peak, top)
        peak = jnp.max(peak, axis=1, keepdims=True)
        total = blended = None
        for i, (side, load) in enumerate(rows(1)):
            p = jnp.exp2(scores[:, 256 * i : 256 * i + 256] - peak)
            part = p[:, :128] + p[:, 128:]
            total = part if total is None else total + part
            o = jnp.dot(p.astype(jnp.bfloat16), load(), preferred_element_type=jnp.float32)
            blended = o if blended is None else blended + o
        total = jnp.sum(total, axis=1, keepdims=True)
        result[k, t] = (blended / total).astype(jnp.bfloat16)

    def out_copy(k, t, half):
        slot = (k + 1) % 4 if half == 0 else k
        py = (y + 4 - slot) % 4
        rows = pl.ds(0, 64) if half == 0 else pl.ds(64, 64)
        there = pl.ds(64, 64) if half == 0 else pl.ds(0, 64)
        return (result.at[k, pl.ds(2 * t, 2), rows], out.at[:, there, lanes(x * 4 + y)], o_send.at[(4 * k + t) * 2 + half], py, slot)

    def out_remote(k, t, half):
        src, dst, ss, py, _ = out_copy(k, t, half)
        return pltpu.make_async_remote_copy(src, dst, ss, o_recv, device_id=source(t, py), device_id_type=MESH)

    def give(k, t):
        for half in (0, 1):
            src, dst, _, _, slot = out_copy(k, t, half)
            if slot == 0:
                mine = (t == ta) & (x_hi == core)

                @pl.when(mine)
                def _():
                    pltpu.make_async_copy(src, dst, o_recv).start()

                @pl.when(jnp.logical_not(mine))
                def _():
                    out_remote(k, t, half).start()
            else:
                out_remote(k, t, half).start()

    def given(k, t):
        for half in (0, 1):
            slot = out_copy(k, t, half)[4]
            if slot == 0:

                @pl.when(jnp.logical_not((t == ta) & (x_hi == core)))
                def _():
                    out_remote(k, t, half).wait_send()
            else:
                out_remote(k, t, half).wait_send()

    for k in range(4):
        forward(k)
    arrived(0)
    for k in range(4):
        if k < 3:
            arrived(k + 1)
        set_bias(k)

        @pl.loop(0, 4)
        def _(t):
            @pl.loop(0, 2)
            def _(f):
                unit(k, 2 * t + f)

            give(k, t)

    for k in range(4):
        exchanged(far_copy, k)
        exchanged(kv_copy, k)
        exchanged(q_copy, k)

        @pl.loop(0, 4)
        def _(t):
            @pl.when(has_right)
            def _():
                halo_copy(k, t, 1).wait_send()

            @pl.when(has_left)
            def _():
                halo_copy(k, t, -1).wait_send()

            given(k, t)

    pltpu.make_async_copy(out, out, o_recv).wait()


def per_device(queries, keyvals, far_frames):
    frames, _, _, features = queries.shape
    q = queries.reshape(frames, ROWS, features)
    kv = keyvals.reshape(2, frames, ROWS, features)
    far = far_frames.reshape(-1)
    cells = [pltpu.VMEM((2, NF, ROWS, HD), jnp.bfloat16)] * 12
    dma = pltpu.SemaphoreType.DMA
    out = pl.pallas_call(
        kernel,
        out_shape=jax.ShapeDtypeStruct(q.shape, jnp.bfloat16),
        in_specs=[pl.BlockSpec(memory_space=pl.ANY)] * 2 + [pl.BlockSpec(memory_space=pltpu.SMEM)],
        out_specs=pl.BlockSpec(memory_space=pl.ANY),
        scratch_shapes=[pltpu.VMEM((NF, ROWS, HD), jnp.bfloat16)] * 4
        + cells
        + [
            pltpu.SMEM((16, 8), jnp.int32),
            pltpu.VMEM((4, ROWS, 2 * ROWS), jnp.float32),
            pltpu.VMEM((ROWS, 2560), jnp.float32),
            pltpu.VMEM((ROWS, 2560), jnp.bfloat16),
            pltpu.VMEM((4, NF, ROWS, HD), jnp.bfloat16),
        ]
        + [dma((16,))] * 6
        + [dma((2, 16))] * 2
        + [dma((32,)), dma],
        compiler_params=pltpu.CompilerParams(collective_id=0, has_side_effects=True, vmem_limit_bytes=56 * 2**20),
        name="tile_attention",
    )(q, kv, far)
    return out.reshape(queries.shape)


def solution(mesh):
    placed = (P("ta", "ha", "wa", None), P(None, "ta", "ha", "wa", None), P("ta", "ha", "wa", None))
    return jax.shard_map(per_device, mesh=mesh, in_specs=placed, out_specs=P("ta", "ha", "wa", None), check_vma=False)
```

time: 545 us -> 91.1 us (0.17)
  the two profiles are of different devices: /device:TPU:1 before, /device:TPU:163 now
where the time goes in v1:
time: 91.1 us; the launch traced here: 90.9 us
  Pallas kernels  86.1 us (95%)
  local copies, waits for them, and re-layouts  3.41 us (4%)
  other arithmetic  1.34 us (1%)
    pallas_call x1, Pallas kernels, per_device(): pl.pallas_call(kernel, out_shape=jax.ShapeDtypeStruct(q.shape, jnp.bfloat...  86.1 us
    unnamed x2, local copies, waits for them, and re-layouts  2.82 us

profile of v1, /device:TPU:163, one launch (start us, length us, event | category | flops | bytes accessed | tf_op | source)
XLA Modules:
  0.0 90.9 jit_solution(14811697696488786669)
XLA Ops:
  0.0 0.5 broadcast.3
  0.5 1.3 %reduce.3 = s32[2,2,2]{2,1,0:T(2,128)S(1)} reduce(s32[2,2,1,2]{3,2,1,0:T(1,128)} %param.5, s32[]{:T(128)} %broadcast.3), dimensions={2}, to_apply=%param.5.reduce_sub_computation.3 | reduce | bytes 68 | tf_op args[2]
  1.9 0.6 reshape.14.far
  2.5 86.1 %tile_attention.1 = bf16[2,128,2048]{2,1,0:T(8,128)(2,1)} custom-call(bf16[2,128,2048]{2,1,0:T(8,128)(2,1)} %bitcast.5, bf16[2,2,128,2048]{3,2,1,0:T(8,128)(2,1)} %bitcast.4, s32[8]{0:T(128)} %reshape.14.far), custom_call_target="tpu_custom_call" | custom-call | tf_op jit(solution)/shard_map/tile_attention/pallas_call | solution.py:303
  88.6 2.3 %copy.5 = bf16[2,16,8,2048]{3,2,1,0:T(8,128)(2,1)} copy(bf16[2,16,8,2048]{3,2,1,0:T(8,128)(2,1)} %bitcast.3) | data formatting | bytes 2097152

commit v2 on v1

--- a/solution.py
+++ b/solution.py
@@ -18,7 +18,8 @@
 
 def kernel(q, kv, far, out, *scratch):
     qs, own, left, right = (scratch[4 * i : 4 * i + 4] for i in range(4))
-    (fars, bias, scores, probs, result, kv_send, kv_recv, q_send, q_recv, f_send, f_recv, z_send, z_recv, o_send, o_recv) = scratch[16:]
+    (fars, bias, *held, result, kv_send, kv_recv, q_send, q_recv, f_send, f_recv, z_send, z_recv, o_send, o_recv) = scratch[16:]
+    scores, peaks = held[:2], held[2:]
     ta, y, wa = lax.axis_index("ta"), lax.axis_index("ha"), lax.axis_index("wa")
     x_lo, core, x_hi, z = ta // 2, ta % 2, wa // 8, wa % 8
     x = x_hi * 2 + x_lo
@@ -69,23 +70,21 @@
         src, dst, ss, rs, px, py = copy
         return pltpu.make_async_remote_copy(src, dst, ss, rs, device_id=place(px, x_hi, py), device_id_type=MESH)
 
-    def exchange(make, k):
-        src, dst, _, rs, _, _ = make(k, 0)
-        if k == 0:
-
-            @pl.when(core == x_hi)
-            def _():
-                pltpu.make_async_copy(src, dst, rs).start()
-
-            @pl.when(core != x_hi)
-            def _():
-                remote(make(k, 0)).start()
-        else:
-            remote(make(k, 0)).start()
-
-        @pl.loop(1, 4)
-        def _(dx):
-            remote(make(k, dx)).start()
+    def exchange(make, *slots):
+        for k, steps in ((0, (0, 1, 3, 2)), (1, (0,)), (3, (0,)), (1, (1,)), (3, (3,)), (1, (3,)), (3, (1,)), (1, (2,)), (3, (2,)), (2, (0, 1, 3, 2))):
+            for dx in steps if k in slots else ():
+                copy = make(k, dx)
+                if k == dx == 0:
+
+                    @pl.when(core == x_hi)
+                    def _():
+                        pltpu.make_async_copy(copy[0], copy[1], copy[3]).start()
+
+                    @pl.when(core != x_hi)
+                    def _():
+                        remote(copy).start()
+                else:
+                    remote(copy).start()
 
     def exchanged(make, k):
         if k == 0:
@@ -100,27 +99,7 @@
         def _(dx):
             remote(make(k, dx)).wait_send()
 
-    for k in range(4):
-        exchange(far_copy, k)
-    exchange(kv_copy, 0)
-    exchange(kv_copy, 1)
-    exchange(q_copy, 0)
-    exchange(q_copy, 1)
-    for k in (2, 3):
-        exchange(kv_copy, k)
-        exchange(q_copy, k)
-
-    @pl.when(column == 0)
-    def _():
-        for ref in left:
-            ref[...] = jnp.zeros_like(ref)
-
-    @pl.when(column == 15)
-    def _():
-        for ref in right:
-            ref[...] = jnp.zeros_like(ref)
-
-    nearer = (((x - 2 * core + 3) % 4) < ((x - 2 * core + 4) % 4)).astype(jnp.int32)
+    nearer = ((x + 4 - 2 * core) % 4 + 1) % 4 // 2
 
     def piece(j):
         return ((nearer + j // 2) % 2) * 2 + j % 2
@@ -137,8 +116,8 @@
             device_id_type=MESH,
         )
 
-    def forward(k):
-        @pl.loop(0, 4)
+    def forward(k, first=0, last=4):
+        @pl.loop(first, last)
         def _(j):
             t = piece(j)
             pltpu.make_async_copy(own[k].at[:, pl.ds(2 * t, 2)], own[k].at[:, pl.ds(2 * t, 2)], kv_recv.at[4 * k + t]).wait()
@@ -148,9 +127,11 @@
                 def _(side=side):
                     halo_copy(k, t, side).start()
 
-    def arrived(k):
-        @pl.loop(0, 4)
-        def _(t):
+    def arrived(k, first=0, last=4):
+        @pl.loop(first, last)
+        def _(j):
+            t = piece(j)
+
             @pl.when(has_left)
             def _():
                 halo_copy(k, t, 1).wait_recv()
@@ -162,56 +143,44 @@
             pltpu.make_async_copy(qs[k].at[pl.ds(2 * t, 2)], qs[k].at[pl.ds(2 * t, 2)], q_recv.at[4 * k + t]).wait()
             pltpu.make_async_copy(far, fars.at[4 * k + t], f_recv.at[4 * k + t]).wait()
 
-    def set_bias(k):
+    def set_bias(k, at=0):
         wraps = (y == k).astype(jnp.int32)
         row = lax.broadcasted_iota(jnp.int32, (ROWS, 2 * ROWS), 0)
         key = lax.broadcasted_iota(jnp.int32, (ROWS, 2 * ROWS), 1)
         half = row // 64
         base = jnp.where((key >= half * (64 + 64 * wraps)) & (key < 192 - 64 * wraps + half * 256), 0.0, NEG).astype(jnp.float32)
-        bias[1] = base
-        bias[0] = jnp.where(has_left, base, NEG)
-        bias[2] = jnp.where(has_right, base, NEG)
-        bias[3] = jnp.where(half == key // 128, 0.0, NEG).astype(jnp.float32)
-
-    def unit(k, t):
+        bias[at + 1] = base
+        bias[at + 0] = jnp.where(has_left, base, NEG)
+        bias[at + 2] = jnp.where(has_right, base, NEG)
+        bias[at + 3] = jnp.where(half == key // 128, 0.0, NEG).astype(jnp.float32)
+
+    def chunks(k, t, kind):
+        low = (k + 1) % 4
+        f_low, f_here, f_at = 4 * low + t // 2, 4 * k + t // 2, (t % 2) * 4
+        distant = [(low, fars[f_low, f_at + 2], 64), (low, fars[f_low, f_at + 3], 64), (k, fars[f_here, f_at], 0), (k, fars[f_here, f_at + 1], 0)]
+
+        def near(cells, f):
+            return lambda: jnp.concatenate([cells[low][kind, f], cells[k][kind, f]], axis=0)
+
+        loads = [(side, near(cells, f)) for side, cells in enumerate((left, own, right)) for f in ((t + 7) % NF, t, (t + 1) % NF)]
+        return loads + [(3, lambda: jnp.concatenate([own[s][kind, f, at : at + 64, :] for s, f, at in distant], axis=0))]
+
+    def score(k, t, held, at):
         low = (k + 1) % 4
         query = jnp.concatenate([qs[low][t, 64:, :], qs[k][t, :64, :]], axis=0)
-        around = [(t + 7) % NF, t, (t + 1) % NF]
-        f_low, f_here = 4 * low + t // 2, 4 * k + t // 2
-        f_at = (t % 2) * 4
-        distant = [fars[f_low, f_at + 2], fars[f_low, f_at + 3], fars[f_here, f_at], fars[f_here, f_at + 1]]
-
-        def rows(kind):
-            chunks = []
-            for side, cells in enumerate((left, own, right)):
-                for f in around:
-                    chunks.append((side, lambda cells=cells, f=f: jnp.concatenate([cells[low][kind, f], cells[k][kind, f]], axis=0)))
-            chunks.append(
-                (
-                    3,
-                    lambda: jnp.concatenate(
-                        [
-                            own[low][kind, distant[0], 64:, :],
-                            own[low][kind, distant[1], 64:, :],
-                            own[k][kind, distant[2], :64, :],
-                            own[k][kind, distant[3], :64, :],
-                        ],
-                        axis=0,
-                    ),
-                )
-            )
-            return chunks
-
         peak = None
-        for i, (side, load) in enumerate(rows(0)):
-            s = lax.dot_general(query, load(), NT, preferred_element_type=jnp.float32) * EXP2_SCALE + bias[side]
-            scores[:, 256 * i : 256 * i + 256] = s
+        for i, (side, load) in enumerate(chunks(k, t, 0)):
+            s = lax.dot_general(query, load(), NT, preferred_element_type=jnp.float32) * EXP2_SCALE + bias[at + side]
+            scores[held][:, 256 * i : 256 * i + 256] = s
             top = jnp.maximum(s[:, :128], s[:, 128:])
             peak = top if peak is None else jnp.maximum(peak, top)
-        peak = jnp.max(peak, axis=1, keepdims=True)
+        peaks[held][...] = peak
+
+    def blend(k, t, held):
+        peak = jnp.max(peaks[held][...], axis=1, keepdims=True)
         total = blended = None
-        for i, (side, load) in enumerate(rows(1)):
-            p = jnp.exp2(scores[:, 256 * i : 256 * i + 256] - peak)
+        for i, (_, load) in enumerate(chunks(k, t, 1)):
+            p = jnp.exp2(scores[held][:, 256 * i : 256 * i + 256] - peak)
             part = p[:, :128] + p[:, 128:]
             total = part if total is None else total + part
             o = jnp.dot(p.astype(jnp.bfloat16), load(), preferred_element_type=jnp.float32)
@@ -219,6 +188,12 @@
         total = jnp.sum(total, axis=1, keepdims=True)
         result[k, t] = (blended / total).astype(jnp.bfloat16)
 
+    def units(k, first, at=0):
+        for held in (0, 1):
+            score(k, (first + held) % NF, held, at)
+        for held in (0, 1):
+            blend(k, (first + held) % NF, held)
+
     def out_copy(k, t, half):
         slot = (k + 1) % 4 if half == 0 else k
         py = (y + 4 - slot) % 4
@@ -257,21 +232,61 @@
             else:
                 out_remote(k, t, half).wait_send()
 
-    for k in range(4):
-        forward(k)
-    arrived(0)
-    for k in range(4):
-        if k < 3:
-            arrived(k + 1)
+    exchange(kv_copy, 0)
+    exchange(kv_copy, 1, 3)
+    exchange(q_copy, 0)
+    @pl.when(column == 0)
+    def _():
+        for ref in left:
+            ref[...] = jnp.zeros_like(ref)
+
+    @pl.when(column == 15)
+    def _():
+        for ref in right:
+            ref[...] = jnp.zeros_like(ref)
+
+    forward(0)
+    exchange(q_copy, 1, 3)
+    exchange(kv_copy, 2)
+    forward(1)
+    exchange(q_copy, 2)
+    exchange(far_copy, 0, 1, 2, 3)
+    forward(3)
+
+    def full(k):
         set_bias(k)
 
         @pl.loop(0, 4)
         def _(t):
-            @pl.loop(0, 2)
-            def _(f):
-                unit(k, 2 * t + f)
-
+            units(k, 2 * t)
             give(k, t)
+
+    forward(2)
+    arrived(0)
+    arrived(1)
+    full(0)
+    arrived(3)
+    full(3)
+    base = 4 * nearer
+    set_bias(1, 0)
+    set_bias(2, 4)
+    arrived(2, 0, 1)
+
+    @pl.loop(1, 4)
+    def _(j):
+        arrived(2, j, j + 1)
+        for k in (1, 2):
+            units(k, base + 2 * j - 1, 4 * k - 4)
+
+        @pl.when(j > 1)
+        def _():
+            for k in (1, 2):
+                give(k, piece(j - 1))
+
+    for k in (1, 2):
+        units(k, base + 7, 4 * k - 4)
+        give(k, piece(3))
+        give(k, piece(0))
 
     for k in range(4):
         exchanged(far_copy, k)
@@ -309,9 +324,11 @@
         + cells
         + [
             pltpu.SMEM((16, 8), jnp.int32),
-            pltpu.VMEM((4, ROWS, 2 * ROWS), jnp.float32),
+            pltpu.VMEM((8, ROWS, 2 * ROWS), jnp.float32),
             pltpu.VMEM((ROWS, 2560), jnp.float32),
-            pltpu.VMEM((ROWS, 2560), jnp.bfloat16),
+            pltpu.VMEM((ROWS, 2560), jnp.float32),
+            pltpu.VMEM((ROWS, HD), jnp.float32),
+            pltpu.VMEM((ROWS, HD), jnp.float32),
             pltpu.VMEM((4, NF, ROWS, HD), jnp.bfloat16),
         ]
         + [dma((16,))] * 6

time: 91.1 us -> 80.5 us (0.88)
  the two profiles are of different devices: /device:TPU:163 before, /device:TPU:1 now
where the time goes in v2:
time: 80.5 us; the launch traced here: 79.5 us
  Pallas kernels  74.8 us (93%)
  local copies, waits for them, and re-layouts  3.41 us (4%)
  other arithmetic  1.34 us (2%)
    pallas_call x1, Pallas kernels, per_device(): pl.pallas_call(kernel, out_shape=jax.ShapeDtypeStruct(q.shape, jnp.bfloat...  74.8 us
    unnamed x2, local copies, waits for them, and re-layouts  2.82 us

profile of v2, /device:TPU:1, one launch (start us, length us, event | category | flops | bytes accessed | tf_op | source)
XLA Modules:
  0.0 79.5 jit_solution(14667093099560222865)
XLA Ops:
  0.0 0.5 broadcast.3
  0.5 1.3 %reduce.3 = s32[2,2,2]{2,1,0:T(2,128)S(1)} reduce(s32[2,2,1,2]{3,2,1,0:T(1,128)} %param.5, s32[]{:T(128)} %broadcast.3), dimensions={2}, to_apply=%param.5.reduce_sub_computation.3 | reduce | bytes 68 | tf_op args[2]
  1.9 0.6 reshape.14.far
  2.5 74.8 %tile_attention.1 = bf16[2,128,2048]{2,1,0:T(8,128)(2,1)} custom-call(bf16[2,128,2048]{2,1,0:T(8,128)(2,1)} %bitcast.5, bf16[2,2,128,2048]{3,2,1,0:T(8,128)(2,1)} %bitcast.4, s32[8]{0:T(128)} %reshape.14.far), custom_call_target="tpu_custom_call" | custom-call | tf_op jit(solution)/shard_map/tile_attention/pallas_call | solution.py:318
  77.2 2.3 %copy.5 = bf16[2,16,8,2048]{3,2,1,0:T(8,128)(2,1)} copy(bf16[2,16,8,2048]{3,2,1,0:T(8,128)(2,1)} %bitcast.3) | data formatting | bytes 2097152

commit v3 on v2

--- a/solution.py
+++ b/solution.py
@@ -194,22 +194,28 @@
         for held in (0, 1):
             blend(k, (first + held) % NF, held)
 
-    def out_copy(k, t, half):
+    def out_copy(k, f, count, half):
         slot = (k + 1) % 4 if half == 0 else k
         py = (y + 4 - slot) % 4
         rows = pl.ds(0, 64) if half == 0 else pl.ds(64, 64)
         there = pl.ds(64, 64) if half == 0 else pl.ds(0, 64)
-        return (result.at[k, pl.ds(2 * t, 2), rows], out.at[:, there, lanes(x * 4 + y)], o_send.at[(4 * k + t) * 2 + half], py, slot)
-
-    def out_remote(k, t, half):
-        src, dst, ss, py, _ = out_copy(k, t, half)
-        return pltpu.make_async_remote_copy(src, dst, ss, o_recv, device_id=source(t, py), device_id_type=MESH)
-
-    def give(k, t):
+        return (
+            result.at[k, pl.ds(f, count), rows],
+            out.at[pl.ds(f % 2, count), there, lanes(x * 4 + y)],
+            o_send.at[(4 * k + f // 2) * 2 + half],
+            py,
+            slot,
+        )
+
+    def out_remote(k, f, count, half):
+        src, dst, ss, py, _ = out_copy(k, f, count, half)
+        return pltpu.make_async_remote_copy(src, dst, ss, o_recv, device_id=source(f // 2, py), device_id_type=MESH)
+
+    def give(k, f, count):
         for half in (0, 1):
-            src, dst, _, _, slot = out_copy(k, t, half)
+            src, dst, _, _, slot = out_copy(k, f, count, half)
             if slot == 0:
-                mine = (t == ta) & (x_hi == core)
+                mine = (f // 2 == ta) & (x_hi == core)
 
                 @pl.when(mine)
                 def _():
@@ -217,24 +223,32 @@
 
                 @pl.when(jnp.logical_not(mine))
                 def _():
-                    out_remote(k, t, half).start()
+                    out_remote(k, f, count, half).start()
             else:
-                out_remote(k, t, half).start()
+                out_remote(k, f, count, half).start()
 
     def given(k, t):
         for half in (0, 1):
-            slot = out_copy(k, t, half)[4]
+            slot = out_copy(k, 2 * t, 2, half)[4]
             if slot == 0:
 
                 @pl.when(jnp.logical_not((t == ta) & (x_hi == core)))
                 def _():
-                    out_remote(k, t, half).wait_send()
+                    out_remote(k, 2 * t, 2, half).wait_send()
             else:
-                out_remote(k, t, half).wait_send()
+                out_remote(k, 2 * t, 2, half).wait_send()
+
+    def full(k):
+        set_bias(k)
+
+        @pl.loop(0, 4)
+        def _(t):
+            units(k, 2 * t)
+            give(k, 2 * t, 2)
 
     exchange(kv_copy, 0)
-    exchange(kv_copy, 1, 3)
-    exchange(q_copy, 0)
+    exchange(far_copy, 0, 1, 2, 3)
+    exchange(kv_copy, 1,3)
     @pl.when(column == 0)
     def _():
         for ref in left:
@@ -246,25 +260,22 @@
             ref[...] = jnp.zeros_like(ref)
 
     forward(0)
-    exchange(q_copy, 1, 3)
     exchange(kv_copy, 2)
+    exchange(q_copy, 0)
     forward(1)
+    exchange(q_copy, 1,3)
+    forward(3)
     exchange(q_copy, 2)
-    exchange(far_copy, 0, 1, 2, 3)
-    forward(3)
-
-    def full(k):
-        set_bias(k)
-
-        @pl.loop(0, 4)
-        def _(t):
-            units(k, 2 * t)
-            give(k, t)
-
-    forward(2)
     arrived(0)
     arrived(1)
-    full(0)
+    set_bias(0)
+
+    @pl.loop(0, 4)
+    def _(t):
+        forward(2, t, t + 1)
+        units(0, 2 * t)
+        give(0, 2 * t, 2)
+
     arrived(3)
     full(3)
     base = 4 * nearer
@@ -272,21 +283,18 @@
     set_bias(2, 4)
     arrived(2, 0, 1)
 
+    def follow(first):
+        for k in (1, 2):
+            units(k, first, 4 * k - 4)
+            for held in (0, 1):
+                give(k, (first + held) % NF, 1)
+
     @pl.loop(1, 4)
     def _(j):
         arrived(2, j, j + 1)
-        for k in (1, 2):
-            units(k, base + 2 * j - 1, 4 * k - 4)
-
-        @pl.when(j > 1)
-        def _():
-            for k in (1, 2):
-                give(k, piece(j - 1))
-
-    for k in (1, 2):
-        units(k, base + 7, 4 * k - 4)
-        give(k, piece(3))
-        give(k, piece(0))
+        follow(base + 2 * j - 1)
+
+    follow(base + 7)
 
     for k in range(4):
         exchanged(far_copy, k)

time: 80.5 us -> 76 us (0.944)
  Pallas kernels: 74.8 us -> 70.8 us
    pallas_call x1, Pallas kernels: 74.8 us -> 70.8 us  [per_device(): pl.pallas_call(kernel, out_shape=jax.ShapeDtypeStruct(q.shape, jnp.bfloat...]
where the time goes in v3:
time: 76 us; the launch traced here: 75.6 us
  Pallas kernels  70.8 us (93%)
  local copies, waits for them, and re-layouts  3.41 us (4%)
  other arithmetic  1.34 us (2%)
    pallas_call x1, Pallas kernels, per_device(): pl.pallas_call(kernel, out_shape=jax.ShapeDtypeStruct(q.shape, jnp.bfloat...  70.8 us
    unnamed x2, local copies, waits for them, and re-layouts  2.82 us

profile of v3, /device:TPU:1, one launch (start us, length us, event | category | flops | bytes accessed | tf_op | source)
XLA Modules:
  0.0 75.6 jit_solution(5100307326937109356)
XLA Ops:
  0.0 0.5 broadcast.3
  0.5 1.3 %reduce.3 = s32[2,2,2]{2,1,0:T(2,128)S(1)} reduce(s32[2,2,1,2]{3,2,1,0:T(1,128)} %param.5, s32[]{:T(128)} %broadcast.3), dimensions={2}, to_apply=%param.5.reduce_sub_computation.3 | reduce | bytes 68 | tf_op args[2]
  1.9 0.6 reshape.14.far
  2.5 70.8 %tile_attention.1 = bf16[2,128,2048]{2,1,0:T(8,128)(2,1)} custom-call(bf16[2,128,2048]{2,1,0:T(8,128)(2,1)} %bitcast.5, bf16[2,2,128,2048]{3,2,1,0:T(8,128)(2,1)} %bitcast.4, s32[8]{0:T(128)} %reshape.14.far), custom_call_target="tpu_custom_call" | custom-call | tf_op jit(solution)/shard_map/tile_attention/pallas_call | solution.py:326
  73.2 2.3 %copy.5 = bf16[2,16,8,2048]{3,2,1,0:T(8,128)(2,1)} copy(bf16[2,16,8,2048]{3,2,1,0:T(8,128)(2,1)} %bitcast.3) | data formatting | bytes 2097152

commit v4 on v3

--- a/solution.py
+++ b/solution.py
@@ -19,7 +19,7 @@
 def kernel(q, kv, far, out, *scratch):
     qs, own, left, right = (scratch[4 * i : 4 * i + 4] for i in range(4))
     (fars, bias, *held, result, kv_send, kv_recv, q_send, q_recv, f_send, f_recv, z_send, z_recv, o_send, o_recv) = scratch[16:]
-    scores, peaks = held[:2], held[2:]
+    scores, peaks = held[:4], held[4:]
     ta, y, wa = lax.axis_index("ta"), lax.axis_index("ha"), lax.axis_index("wa")
     x_lo, core, x_hi, z = ta // 2, ta % 2, wa // 8, wa % 8
     x = x_hi * 2 + x_lo
@@ -241,10 +241,14 @@
     def full(k):
         set_bias(k)
 
-        @pl.loop(0, 4)
-        def _(t):
-            units(k, 2 * t)
-            give(k, 2 * t, 2)
+        @pl.loop(0, 2)
+        def _(i):
+            for f in range(4):
+                score(k, 4 * i + f, f, 0)
+            for f in range(4):
+                blend(k, 4 * i + f, f)
+            give(k, 4 * i, 2)
+            give(k, 4 * i + 2, 2)
 
     exchange(kv_copy, 0)
     exchange(far_copy, 0, 1, 2, 3)
@@ -284,10 +288,13 @@
     arrived(2, 0, 1)
 
     def follow(first):
-        for k in (1, 2):
-            units(k, first, 4 * k - 4)
-            for held in (0, 1):
-                give(k, (first + held) % NF, 1)
+        steps = [(k, (first + f) % NF, 2 * k - 2 + f) for k in (1, 2) for f in (0, 1)]
+        for k, f, held in steps:
+            score(k, f, held, 4 * k - 4)
+        for k, f, held in steps:
+            blend(k, f, held)
+        for k, f, _ in steps:
+            give(k, f, 1)
 
     @pl.loop(1, 4)
     def _(j):
@@ -333,10 +340,8 @@
         + [
             pltpu.SMEM((16, 8), jnp.int32),
             pltpu.VMEM((8, ROWS, 2 * ROWS), jnp.float32),
-            pltpu.VMEM((ROWS, 2560), jnp.float32),
-            pltpu.VMEM((ROWS, 2560), jnp.float32),
-            pltpu.VMEM((ROWS, HD), jnp.float32),
-            pltpu.VMEM((ROWS, HD), jnp.float32),
+            *[pltpu.VMEM((ROWS, 2560), jnp.float32)] * 4,
+            *[pltpu.VMEM((ROWS, HD), jnp.float32)] * 4,
             pltpu.VMEM((4, NF, ROWS, HD), jnp.bfloat16),
         ]
         + [dma((16,))] * 6

time: 76 us -> 75.8 us (level)
  no operation moved by 1% of the time
where the time goes in v4:
time: 75.8 us; the launch traced here: 75.6 us
  Pallas kernels  70.8 us (93%)
  local copies, waits for them, and re-layouts  3.41 us (4%)
  other arithmetic  1.34 us (2%)
    pallas_call x1, Pallas kernels, per_device(): pl.pallas_call(kernel, out_shape=jax.ShapeDtypeStruct(q.shape, jnp.bfloat...  70.8 us
    unnamed x2, local copies, waits for them, and re-layouts  2.82 us

profile of v4, /device:TPU:1, one launch (start us, length us, event | category | flops | bytes accessed | tf_op | source)
XLA Modules:
  0.0 75.6 jit_solution(17264884607699281666)
XLA Ops:
  0.0 0.5 broadcast.3
  0.5 1.3 %reduce.3 = s32[2,2,2]{2,1,0:T(2,128)S(1)} reduce(s32[2,2,1,2]{3,2,1,0:T(1,128)} %param.5, s32[]{:T(128)} %broadcast.3), dimensions={2}, to_apply=%param.5.reduce_sub_computation.3 | reduce | bytes 68 | tf_op args[2]
  1.9 0.6 reshape.14.far
  2.5 70.8 %tile_attention.1 = bf16[2,128,2048]{2,1,0:T(8,128)(2,1)} custom-call(bf16[2,128,2048]{2,1,0:T(8,128)(2,1)} %bitcast.5, bf16[2,2,128,2048]{3,2,1,0:T(8,128)(2,1)} %bitcast.4, s32[8]{0:T(128)} %reshape.14.far), custom_call_target="tpu_custom_call" | custom-call | tf_op jit(solution)/shard_map/tile_attention/pallas_call | solution.py:333
  73.3 2.3 %copy.5 = bf16[2,16,8,2048]{3,2,1,0:T(8,128)(2,1)} copy(bf16[2,16,8,2048]{3,2,1,0:T(8,128)(2,1)} %bitcast.3) | data formatting | bytes 2097152
